TPU v7x, 32 devices: a whole 2x2x4 slice. The times are simulated.
32 devices in a mesh: groups: 2 (over x), tokens: 16 (over z, y, core).
Axes of the slice: x: 2, y: 2, z: 4, core: 2. Of those that a mesh axis runs over, the one named last changes fastest.
Arguments:
- text_query: bfloat16 [256, 2, 1280], P(('groups', 'tokens')), parts along dimension 0, may hold values from -6 to 6
- frame_key: bfloat16 [16384, 2, 1280], P(('groups', 'tokens')), parts along dimension 0, may hold values from -6 to 6
- frame_value: bfloat16 [16384, 2560], P(('groups', 'tokens')), parts along dimension 0, may hold values from -6 to 6
- forward_out: bfloat16 [256, 2, 2560], P(('groups', 'tokens')), parts along dimension 0, may hold values from -3 to 3
- out_grad: bfloat16 [256, 2560], P(('groups', 'tokens')), parts along dimension 0, may hold values from -1536 to 1536
- log_norms: float32 [256, 2, 10], P(('groups', 'tokens')), parts along dimension 0, as said below
- lambdas: float32 [10], replicated, may hold values from 0.2 to 0.8
- visits: int32 [32, 12], P('groups'), parts along dimension 0, may hold values from 0 to 15, all different within a row; in each aligned block of 16 rows (0 to 15, 16 to 31, ...) at most 14 rows name the same one
- bounds: int32 [32], P('groups'), parts along dimension 0, may hold values from 2 to 6, as said below
- text_count: int32 [1], replicated, may hold values from 64 to 128
Outputs:
- query_grad: bfloat16 [256, 2, 1280], P(('groups', 'tokens')), parts along dimension 0
- key_grad: bfloat16 [16384, 2, 1280], P(('groups', 'tokens')), parts along dimension 0
- value_grad: bfloat16 [16384, 2560], P(('groups', 'tokens')), parts along dimension 0
There are 2 independent parts, one for each index of `groups`. A program takes and returns all parts, laid end to end along the dimension named above; an argument that names none is the same for every part. Nothing has to cross between parts.
Inputs may be any that keep to these rules, and one draw needn't show every extreme that they name: `visits`: row b lists 6 frame shards for the first segment of text block b and then 6 for its second, all 12 different; every shard is listed by at most 14 blocks, a bound that some block reaches. Segment 1 of text block b begins at its row bounds[b]; some block has bounds 2 and some has 6, so no segment is longer than 6 rows. Text rows from text_count onward are padding in every group. `log_norms`: each entry lies within 1.5 of the logarithm of 3072.
All inputs are finite; a program needn't handle non-finite values.
Results may differ from a plain program's by a relative error of at most 0.005.
Values may be sent and summed in bfloat16 or wider, within the bound.
A program may use at most 128 MiB of HBM per device.

v0:
```python
import jax
import jax.numpy as jnp
from jax import lax
from jax.sharding import PartitionSpec as P


def segment_slots(in_first, in_second, bound_vals, block_ids, capacity, text_rows, text_count):
    start_row = jnp.where(in_second, bound_vals, 0)
    seg_length = jnp.where(in_first, bound_vals, jnp.where(in_second, text_rows - bound_vals, 0))
    slot_index = jnp.arange(capacity, dtype=jnp.int32)
    local_rows = start_row[:, None] + slot_index[None, :]
    global_rows = block_ids[:, None] * text_rows + local_rows
    used = jnp.logical_and(slot_index[None, :] < seg_length[:, None], global_rows < text_count[0])
    safe_rows = jnp.minimum(local_rows, text_rows - 1)
    return (safe_rows, used.astype(jnp.float32))


def place_rows(local_rows, used, text_rows):
    row_ids = jnp.arange(text_rows, dtype=jnp.int32)
    return (local_rows[:, :, None] == row_ids[None, None, :]).astype(jnp.float32) * used[:, :, None]


def visit_rows(
    query_rows,
    grad_rows,
    norm_rows,
    slope_rows,
    live_mask,
    frame_key,
    frame_value,
    lambdas,
    key_acc,
    value_acc,
):
    head_count = lambdas.shape[0]
    key_size = frame_key.shape[2] // head_count
    value_size = frame_value.shape[1] // head_count
    score_scale = float(key_size) ** (-0.5)
    part_rows = query_rows.shape[0]

    def head_step(head_index, running):
        key_total, value_total, query_part = running
        q_head = lax.dynamic_slice_in_dim(query_rows, head_index * key_size, key_size, 2)
        k_head = lax.dynamic_slice_in_dim(frame_key, head_index * key_size, key_size, 2)
        v_head = lax.dynamic_slice_in_dim(frame_value, head_index * value_size, value_size, 1)
        g_head = lax.dynamic_slice_in_dim(grad_rows, head_index * value_size, value_size, 1)
        norm_head = lax.dynamic_index_in_dim(norm_rows, head_index, 2, keepdims=False)
        slope_head = lax.dynamic_index_in_dim(slope_rows, head_index, 2, keepdims=False)
        weight_two = lax.dynamic_index_in_dim(lambdas, head_index, 0, keepdims=False)
        spread = jnp.dot(g_head, v_head.T, preferred_element_type=jnp.float32)
        score_one = (
            jnp.dot(q_head[:, 0], k_head[:, 0].T, preferred_element_type=jnp.float32) * score_scale
        )
        score_two = (
            jnp.dot(q_head[:, 1], k_head[:, 1].T, preferred_element_type=jnp.float32) * score_scale
        )
        prob_one = live_mask[:, None] * jnp.exp(score_one - norm_head[:, 0:1])
        prob_two = live_mask[:, None] * jnp.exp(score_two - norm_head[:, 1:2])
        grad_one = (prob_one * (spread - slope_head[:, 0:1])).astype(jnp.bfloat16)
        grad_two = (prob_two * (-weight_two * spread - slope_head[:, 1:2])).astype(jnp.bfloat16)
        mixed_weight = (prob_one - weight_two * prob_two).astype(jnp.bfloat16)
        value_new = jnp.dot(mixed_weight.T, g_head, preferred_element_type=jnp.float32)
        key_new = (
            jnp.stack(
                [
                    jnp.dot(grad_one.T, q_head[:, 0], preferred_element_type=jnp.float32),
                    jnp.dot(grad_two.T, q_head[:, 1], preferred_element_type=jnp.float32),
                ],
                axis=1,
            )
            * score_scale
        )
        query_new = (
            jnp.stack(
                [
                    jnp.dot(grad_one, k_head[:, 0], preferred_element_type=jnp.float32),
                    jnp.dot(grad_two, k_head[:, 1], preferred_element_type=jnp.float32),
                ],
                axis=1,
            )
            * score_scale
        )
        key_old = lax.dynamic_slice_in_dim(key_total, head_index * key_size, key_size, 2)
        key_total = lax.dynamic_update_slice_in_dim(
            key_total, key_old + key_new, head_index * key_size, 2
        )
        value_old = lax.dynamic_slice_in_dim(value_total, head_index * value_size, value_size, 1)
        value_total = lax.dynamic_update_slice_in_dim(
            value_total, value_old + value_new, head_index * value_size, 1
        )
        query_part = lax.dynamic_update_slice_in_dim(
            query_part, query_new, head_index * key_size, 2
        )
        return (key_total, value_total, query_part)

    query_start = jnp.zeros((part_rows,) + query_rows.shape[1:], jnp.float32)
    return lax.fori_loop(0, head_count, head_step, (key_acc, value_acc, query_start))


def per_device(
    text_query,
    frame_key,
    frame_value,
    forward_out,
    out_grad,
    log_norms,
    lambdas,
    visits,
    bounds,
    text_count,
):
    shard_count = lax.axis_size("tokens")
    my_index = lax.axis_index("tokens")
    text_rows = text_query.shape[0]
    head_count = lambdas.shape[0]
    value_size = frame_value.shape[1] // head_count
    visit_width = visits.shape[1] // 2
    capacity = 3 * text_rows // 4
    grads_wide = out_grad.astype(jnp.float32).reshape(text_rows, head_count, value_size)
    outs_wide = forward_out.astype(jnp.float32).reshape(text_rows, 2, head_count, value_size)
    map_coefs = jnp.stack([jnp.ones_like(lambdas), -lambdas])
    slopes = jnp.sum(grads_wide[:, None] * outs_wide, axis=3) * map_coefs[None]
    all_norms, all_slopes = (
        lax.all_gather(log_norms, "tokens", axis=0, tiled=True),
        lax.all_gather(slopes, "tokens", axis=0, tiled=True),
    )
    zero_keys = jnp.zeros(frame_key.shape, jnp.float32)
    zero_values = jnp.zeros(frame_value.shape, jnp.float32)
    shards = jnp.arange(shard_count, dtype=jnp.int32)
    query_shape = text_query.shape[1:]
    flat_width = query_shape[0] * query_shape[1]
    my_list = lax.dynamic_index_in_dim(visits, my_index, 0, keepdims=False)
    my_bound = lax.dynamic_index_in_dim(bounds, my_index, 0, keepdims=False)
    send_first = jnp.any(my_list[:visit_width][None, :] == shards[:, None], axis=1)
    send_second = jnp.any(my_list[visit_width:][None, :] == shards[:, None], axis=1)
    send_rows, send_used = segment_slots(
        send_first,
        send_second,
        jnp.broadcast_to(my_bound, (shard_count,)),
        jnp.broadcast_to(my_index, (shard_count,)),
        capacity,
        text_rows,
        text_count,
    )
    recv_first = jnp.any(visits[:, :visit_width] == my_index, axis=1)
    recv_second = jnp.any(visits[:, visit_width:] == my_index, axis=1)
    recv_rows, recv_used = segment_slots(
        recv_first, recv_second, bounds, shards, capacity, text_rows, text_count
    )
    flat_send = send_rows.reshape(-1)
    sent_query = jnp.take(text_query, flat_send, axis=0)
    sent_grad = jnp.take(out_grad, flat_send, axis=0)
    got_query, got_grad = (
        lax.all_to_all(sent_query, "tokens", split_axis=0, concat_axis=0, tiled=True),
        lax.all_to_all(sent_grad, "tokens", split_axis=0, concat_axis=0, tiled=True),
    )
    global_recv = (shards[:, None] * text_rows + recv_rows).reshape(-1)
    norm_rows = jnp.take(all_norms, global_recv, axis=0)
    slope_rows = jnp.take(all_slopes, global_recv, axis=0)
    key_acc, value_acc, query_part = visit_rows(
        got_query,
        got_grad,
        norm_rows,
        slope_rows,
        recv_used.reshape(-1),
        frame_key,
        frame_value,
        lambdas,
        zero_keys,
        zero_values,
    )
    came_back = lax.all_to_all(query_part, "tokens", split_axis=0, concat_axis=0, tiled=True)
    grouped = came_back.reshape(shard_count, came_back.shape[0] // shard_count, flat_width)
    placing = place_rows(send_rows, send_used, text_rows)
    query_sum = jnp.einsum(
        "jsx,jsc->xc", placing, grouped, precision=lax.Precision.HIGHEST
    ).reshape((text_rows,) + query_shape)
    return (
        query_sum.astype(jnp.bfloat16),
        key_acc.astype(jnp.bfloat16),
        value_acc.astype(jnp.bfloat16),
    )


def solution(mesh):
    return jax.shard_map(
        per_device,
        mesh=mesh,
        in_specs=(
            P(("groups", "tokens"), None, None),
            P(("groups", "tokens"), None, None),
            P(("groups", "tokens"), None),
            P(("groups", "tokens"), None, None),
            P(("groups", "tokens"), None),
            P(("groups", "tokens"), None, None),
            P(),
            P("groups", None),
            P("groups"),
            P(),
        ),
        out_specs=(
            P(("groups", "tokens"), None, None),
            P(("groups", "tokens"), None, None),
            P(("groups", "tokens"), None),
        ),
        check_vma=False,
    )
```

profile of v0, /device:TPU:0, one launch (start us, length us, event | category | flops | bytes accessed | tf_op | source)
XLA Modules:
  0.0 242.6 jit_solution(16591408216141167793)
XLA Ops:
  5.0 2.1 gather_fusion.1
  8.4 7.4 %all-to-all-start.1 = ((bf16[16,6,2560]{2,1,0:T(8,128)(2,1)}), bf16[16,6,2560]{2,1,0:T(8,128)(2,1)S(1)}, u32[]{:S(2)}, u32[]{:S(2)}) async-start(bf16[16,6,2560]{2,1,0:T(8,128)(2,1)} %broadcast_select_fusion.1), calls=%async_computation.1 | async-start | bytes 1310720 | tf_op jit(solution)/shard_map/all_to_all | solution.py:155
  19.5 12.9 %all-to-all-done.1 = bf16[16,6,2560]{2,1,0:T(8,128)(2,1)S(1)} async-done(((bf16[16,6,2560]{2,1,0:T(8,128)(2,1)}), bf16[16,6,2560]{2,1,0:T(8,128)(2,1)S(1)}, u32[]{:S(2)}, u32[]{:S(2)}) %all-to-all-start.1) | async-done | bytes 491552 | tf_op jit(solution)/shard_map/all_to_all | solution.py:155
  32.4 4.8 %all-to-all-start = ((bf16[96,2,1280]{2,1,0:T(2,128)(2,1)}), bf16[96,2,1280]{2,1,0:T(2,128)(2,1)S(1)}, u32[]{:S(2)}, u32[]{:S(2)}) async-start(bf16[96,2,1280]{2,1,0:T(2,128)(2,1)} %broadcast_select_fusion), calls=%async_computation | async-start | bytes 983040 | tf_op jit(solution)/shard_map/all_to_all | solution.py:154
  37.2 24.8 %all_gather.6 = f32[128,2,10]{2,1,0:T(2,128)S(1)} all-gather(f32[8,2,10]{2,1,0:T(2,128)S(1)} %copy-done.4), channel_id=1, replica_groups=mesh['groups'=2,'tokens'=16] {'tokens'}, dimensions={0}, use_global_device_ids=true | all-gather | bytes 10880 | tf_op jit(solution)/shard_map/all_gather | solution.py:124
  62.8 19.0 %all_gather.7 = f32[128,2,10]{2,1,0:T(2,128)S(1)} all-gather(f32[8,2,10]{2,1,0:T(2,128)S(1)} %copy.61), channel_id=1, replica_groups=mesh['groups'=2,'tokens'=16] {'tokens'}, dimensions={0}, use_global_device_ids=true | all-gather | bytes 10880 | tf_op jit(solution)/shard_map/all_gather | solution.py:125
  84.2 3.0 %broadcast_in_dim.72 = f32[512,2560]{1,0:T(8,128)} broadcast(f32[]{:T(128)} %constant.125.clone.1), dimensions={} | broadcast | bytes 5242884 | tf_op jit(solution)/shard_map/broadcast_in_dim | solution.py:128
  87.2 3.6 %broadcast_in_dim.71.clone = f32[512,2,1280]{2,1,0:T(2,128)} broadcast(f32[]{:T(128)} %constant.125.clone.1), dimensions={} | broadcast | bytes 5242884 | tf_op jit(solution)/shard_map/broadcast_in_dim | solution.py:127
  90.9 122.9 %while.18 = (s32[]{:T(128)}, f32[512,2,1280]{2,1,0:T(2,128)}, f32[512,2560]{1,0:T(8,128)}, f32[96,2,1280]{2,1,0:T(2,128)}, bf16[96,2,1280]{2,1,0:T(2,128)(2,1)S(...) while((s32[]{:T(128)}, f32[512,2,1280]{2,1,0:T(2,128)}, ...), condition=%wide.region_6.8_spmd.clone, body=%wide.region_5.7_spmd.clone.sunk | while | flops 127189576 | bytes 9318833 | solution.py:97
  94.3 1.6 constant_dynamic-slice_fusion.11
  100.3 2.8 %fusion.66 = f32[512,2560]{1,0:T(8,128)} fusion(f32[512,2560]{1,0:T(8,128)} %get-tuple-element.518, s32[]{:T(128)S(6)} %select_n.149, f32[96,512]{1,0:T(8,128)S(1)} %get-tuple-element.493, f32[96,512]{1,0:T(8,128)S(1)} %fusion.64, f32[]{:T(128)} %bitcast.109, bf16[96,2560]{1,0:T(8,128)(2,1)S(1)} %get-tuple-element.545), kind=kOutput, calls=%fused_computation.6.clone.1 | convolution fusion | flops 25444352 | bytes 1492480 | tf_op jit(solution)/shard_map/while/body/eval_jaxpr/dot_general | solution.py:62
  106.5 1.6 constant_dynamic-slice_fusion.11
  112.5 2.9 %fusion.66 = f32[512,2560]{1,0:T(8,128)} fusion(f32[512,2560]{1,0:T(8,128)} %get-tuple-element.518, s32[]{:T(128)S(6)} %select_n.149, f32[96,512]{1,0:T(8,128)S(1)} %get-tuple-element.493, f32[96,512]{1,0:T(8,128)S(1)} %fusion.64, f32[]{:T(128)} %bitcast.109, bf16[96,2560]{1,0:T(8,128)(2,1)S(1)} %get-tuple-element.545), kind=kOutput, calls=%fused_computation.6.clone.1 | convolution fusion | flops 25444352 | bytes 1492480 | tf_op jit(solution)/shard_map/while/body/eval_jaxpr/dot_general | solution.py:62
  118.8 1.7 constant_dynamic-slice_fusion.11
  124.9 2.8 %fusion.66 = f32[512,2560]{1,0:T(8,128)} fusion(f32[512,2560]{1,0:T(8,128)} %get-tuple-element.518, s32[]{:T(128)S(6)} %select_n.149, f32[96,512]{1,0:T(8,128)S(1)} %get-tuple-element.493, f32[96,512]{1,0:T(8,128)S(1)} %fusion.64, f32[]{:T(128)} %bitcast.109, bf16[96,2560]{1,0:T(8,128)(2,1)S(1)} %get-tuple-element.545), kind=kOutput, calls=%fused_computation.6.clone.1 | convolution fusion | flops 25444352 | bytes 1492480 | tf_op jit(solution)/shard_map/while/body/eval_jaxpr/dot_general | solution.py:62
  131.1 1.7 constant_dynamic-slice_fusion.11
  137.2 2.8 %fusion.66 = f32[512,2560]{1,0:T(8,128)} fusion(f32[512,2560]{1,0:T(8,128)} %get-tuple-element.518, s32[]{:T(128)S(6)} %select_n.149, f32[96,512]{1,0:T(8,128)S(1)} %get-tuple-element.493, f32[96,512]{1,0:T(8,128)S(1)} %fusion.64, f32[]{:T(128)} %bitcast.109, bf16[96,2560]{1,0:T(8,128)(2,1)S(1)} %get-tuple-element.545), kind=kOutput, calls=%fused_computation.6.clone.1 | convolution fusion | flops 25444352 | bytes 1492480 | tf_op jit(solution)/shard_map/while/body/eval_jaxpr/dot_general | solution.py:62
  143.4 1.6 constant_dynamic-slice_fusion.11
  149.5 2.8 %fusion.66 = f32[512,2560]{1,0:T(8,128)} fusion(f32[512,2560]{1,0:T(8,128)} %get-tuple-element.518, s32[]{:T(128)S(6)} %select_n.149, f32[96,512]{1,0:T(8,128)S(1)} %get-tuple-element.493, f32[96,512]{1,0:T(8,128)S(1)} %fusion.64, f32[]{:T(128)} %bitcast.109, bf16[96,2560]{1,0:T(8,128)(2,1)S(1)} %get-tuple-element.545), kind=kOutput, calls=%fused_computation.6.clone.1 | convolution fusion | flops 25444352 | bytes 1492480 | tf_op jit(solution)/shard_map/while/body/eval_jaxpr/dot_general | solution.py:62
  155.7 1.7 constant_dynamic-slice_fusion.11
  161.8 2.8 %fusion.66 = f32[512,2560]{1,0:T(8,128)} fusion(f32[512,2560]{1,0:T(8,128)} %get-tuple-element.518, s32[]{:T(128)S(6)} %select_n.149, f32[96,512]{1,0:T(8,128)S(1)} %get-tuple-element.493, f32[96,512]{1,0:T(8,128)S(1)} %fusion.64, f32[]{:T(128)} %bitcast.109, bf16[96,2560]{1,0:T(8,128)(2,1)S(1)} %get-tuple-element.545), kind=kOutput, calls=%fused_computation.6.clone.1 | convolution fusion | flops 25444352 | bytes 1492480 | tf_op jit(solution)/shard_map/while/body/eval_jaxpr/dot_general | solution.py:62
  168.0 1.7 constant_dynamic-slice_fusion.11
  174.1 2.8 %fusion.66 = f32[512,2560]{1,0:T(8,128)} fusion(f32[512,2560]{1,0:T(8,128)} %get-tuple-element.518, s32[]{:T(128)S(6)} %select_n.149, f32[96,512]{1,0:T(8,128)S(1)} %get-tuple-element.493, f32[96,512]{1,0:T(8,128)S(1)} %fusion.64, f32[]{:T(128)} %bitcast.109, bf16[96,2560]{1,0:T(8,128)(2,1)S(1)} %get-tuple-element.545), kind=kOutput, calls=%fused_computation.6.clone.1 | convolution fusion | flops 25444352 | bytes 1492480 | tf_op jit(solution)/shard_map/while/body/eval_jaxpr/dot_general | solution.py:62
  180.3 1.7 constant_dynamic-slice_fusion.11
  186.4 2.8 %fusion.66 = f32[512,2560]{1,0:T(8,128)} fusion(f32[512,2560]{1,0:T(8,128)} %get-tuple-element.518, s32[]{:T(128)S(6)} %select_n.149, f32[96,512]{1,0:T(8,128)S(1)} %get-tuple-element.493, f32[96,512]{1,0:T(8,128)S(1)} %fusion.64, f32[]{:T(128)} %bitcast.109, bf16[96,2560]{1,0:T(8,128)(2,1)S(1)} %get-tuple-element.545), kind=kOutput, calls=%fused_computation.6.clone.1 | convolution fusion | flops 25444352 | bytes 1492480 | tf_op jit(solution)/shard_map/while/body/eval_jaxpr/dot_general | solution.py:62
  192.6 1.7 constant_dynamic-slice_fusion.11
  198.7 2.8 %fusion.66 = f32[512,2560]{1,0:T(8,128)} fusion(f32[512,2560]{1,0:T(8,128)} %get-tuple-element.518, s32[]{:T(128)S(6)} %select_n.149, f32[96,512]{1,0:T(8,128)S(1)} %get-tuple-element.493, f32[96,512]{1,0:T(8,128)S(1)} %fusion.64, f32[]{:T(128)} %bitcast.109, bf16[96,2560]{1,0:T(8,128)(2,1)S(1)} %get-tuple-element.545), kind=kOutput, calls=%fused_computation.6.clone.1 | convolution fusion | flops 25444352 | bytes 1492480 | tf_op jit(solution)/shard_map/while/body/eval_jaxpr/dot_general | solution.py:62
  210.9 2.8 %fusion.66 = f32[512,2560]{1,0:T(8,128)} fusion(f32[512,2560]{1,0:T(8,128)} %get-tuple-element.518, s32[]{:T(128)S(6)} %select_n.149, f32[96,512]{1,0:T(8,128)S(1)} %get-tuple-element.493, f32[96,512]{1,0:T(8,128)S(1)} %fusion.64, f32[]{:T(128)} %bitcast.109, bf16[96,2560]{1,0:T(8,128)(2,1)S(1)} %get-tuple-element.545), kind=kOutput, calls=%fused_computation.6.clone.1 | convolution fusion | flops 25444352 | bytes 1492480 | tf_op jit(solution)/shard_map/while/body/eval_jaxpr/dot_general | solution.py:62
  213.7 4.0 %all-to-all-start.2 = ((f32[96,2,1280]{2,1,0:T(2,128)}), f32[96,2,1280]{2,1,0:T(2,128)S(1)}, u32[]{:S(2)}, u32[]{:S(2)}) async-start(f32[96,2,1280]{2,1,0:T(2,128)} %get-tuple-element.205), calls=%async_computation.2 | async-start | bytes 1966080 | tf_op jit(solution)/shard_map/all_to_all | solution.py:172
  217.9 5.9 %convert_element_type.46 = bf16[512,2,1280]{2,1,0:T(2,128)(2,1)} convert(f32[512,2,1280]{2,1,0:T(2,128)} %get-tuple-element.206) | non-fusion elementwise | flops 1310720 | bytes 7864320 | tf_op jit(solution)/shard_map/convert_element_type | solution.py:180
  223.8 1.8 convert_element_type.47
  225.6 13.8 %all-to-all-done.2 = f32[96,2,1280]{2,1,0:T(2,128)S(1)} async-done(((f32[96,2,1280]{2,1,0:T(2,128)}), f32[96,2,1280]{2,1,0:T(2,128)S(1)}, u32[]{:S(2)}, u32[]{:S(2)}) %all-to-all-start.2) | async-done | bytes 983072 | tf_op jit(solution)/shard_map/all_to_all | solution.py:172
  (255 shorter events, 86.5 us)
Async XLA Ops:
  0.6 15.7 %copy-start = (bf16[8,2,1280]{2,1,0:T(2,128)(2,1)S(1)}, bf16[8,2,1280]{2,1,0:T(2,128)(2,1)}, u32[]{:S(2)}) copy-start(bf16[8,2,1280]{2,1,0:T(2,128)(2,1)} %param.14) | copy-start | bytes 122884
  0.6 15.3 %copy-start.5 = (s32[16]{0:T(128)S(1)}, s32[16]{0:T(128)}, u32[]{:S(2)}) copy-start(s32[16]{0:T(128)} %param.22) | copy-start | bytes 196
  0.7 15.1 %copy-start.3 = (s32[16,12]{1,0:T(8,128)S(1)}, s32[16,12]{1,0:T(8,128)}, u32[]{:S(2)}) copy-start(s32[16,12]{1,0:T(8,128)} %param.21) | copy-start | bytes 2308
  0.7 15.6 %copy-start.1 = (bf16[8,2560]{1,0:T(8,128)(2,1)S(1)}, bf16[8,2560]{1,0:T(8,128)(2,1)}, u32[]{:S(2)}) copy-start(bf16[8,2560]{1,0:T(8,128)(2,1)} %param.18) | copy-start | bytes 122884
  0.7 15.4 %copy-start.6 = (f32[10]{0:T(128)S(1)}, f32[10]{0:T(128)}, u32[]{:S(2)}) copy-start(f32[10]{0:T(128)} %param.20) | copy-start | bytes 124
  0.7 15.6 %copy-start.2 = (bf16[8,2,2560]{2,1,0:T(2,128)(2,1)S(1)}, bf16[8,2,2560]{2,1,0:T(2,128)(2,1)}, u32[]{:S(2)}) copy-start(bf16[8,2,2560]{2,1,0:T(2,128)(2,1)} %param.17) | copy-start | bytes 245764
  5.0 32.2 %copy-start.4 = (f32[8,2,10]{2,1,0:T(2,128)S(1)}, f32[8,2,10]{2,1,0:T(2,128)}, u32[]{:S(2)}) copy-start(f32[8,2,10]{2,1,0:T(2,128)} %param.19) | copy-start | bytes 1924
  8.4 24.0 %all-to-all-start.1 = ((bf16[16,6,2560]{2,1,0:T(8,128)(2,1)}), bf16[16,6,2560]{2,1,0:T(8,128)(2,1)S(1)}, u32[]{:S(2)}, u32[]{:S(2)}) async-start(bf16[16,6,2560]{2,1,0:T(8,128)(2,1)} %broadcast_select_fusion.1), calls=%async_computation.1 | async-start | bytes 1310720 | tf_op jit(solution)/shard_map/all_to_all | solution.py:155
  32.4 50.6 %all-to-all-start = ((bf16[96,2,1280]{2,1,0:T(2,128)(2,1)}), bf16[96,2,1280]{2,1,0:T(2,128)(2,1)S(1)}, u32[]{:S(2)}, u32[]{:S(2)}) async-start(bf16[96,2,1280]{2,1,0:T(2,128)(2,1)} %broadcast_select_fusion), calls=%async_computation | async-start | bytes 983040 | tf_op jit(solution)/shard_map/all_to_all | solution.py:154
  213.7 10.1 %slice-start = ((s8[5242880]{0:T(1024)(128)(4,1)}), s8[1048576]{0:T(1024)(128)(4,1)S(1)}, s32[]{:S(2)}) async-start(s8[5242880]{0:T(1024)(128)(4,1)} %bitcast.112), calls=%async_computation.3 | async-start | bytes 2097152
  213.7 25.6 %all-to-all-start.2 = ((f32[96,2,1280]{2,1,0:T(2,128)}), f32[96,2,1280]{2,1,0:T(2,128)S(1)}, u32[]{:S(2)}, u32[]{:S(2)}) async-start(f32[96,2,1280]{2,1,0:T(2,128)} %get-tuple-element.205), calls=%async_computation.2 | async-start | bytes 1966080 | tf_op jit(solution)/shard_map/all_to_all | solution.py:172
  217.9 5.9 %slice-start.1 = ((s8[5242880]{0:T(1024)(128)(4,1)}), s8[4194304]{0:T(1024)(128)(4,1)S(1)}, s32[]{:S(2)}) async-start(s8[5242880]{0:T(1024)(128)(4,1)} %bitcast.112), calls=%async_computation.4 | async-start | bytes 8388608
where the time goes:
time: 246 us; the launch traced here: 243 us
  local copies, waits for them, and re-layouts  74.1 us (30%)
  matrix products  52.4 us (21%)
  blocking collectives  43.8 us (18%)
  waiting for transfers between devices  26.7 us (11%)
  other arithmetic  19.5 us (8%)
  starting transfers between devices  16.1 us (7%)
  loops' own time  7.6 us (3%)
    dot_general x10, matrix products, head_step(): jnp.dot(mixed_weight.T, g_head, preferred_element_type=jnp.float32)  28 us
    all_gather x1, blocking collectives, per_device(): lax.all_gather(log_norms, 'tokens', axis=0, tiled=True)  24.8 us
    all_gather x1, blocking collectives, per_device(): lax.all_gather(slopes, 'tokens', axis=0, tiled=True)  19 us
    slice x10, local copies, waits for them, and re-layouts, head_step(): k_head[:, 0]  16.7 us
    all_to_all x1, waiting for transfers between devices, per_device(): lax.all_to_all(query_part, 'tokens', split_axis=0, concat_axis=0, tiled=T...  13.8 us
    all_to_all x1, waiting for transfers between devices, per_device(): lax.all_to_all(sent_grad, 'tokens', split_axis=0, concat_axis=0, tiled=True)  12.9 us
    dynamic_update_slice x10, local copies, waits for them, and re-layouts, head_step(): lax.dynamic_update_slice_in_dim(key_total, key_old + key_new, head_index...  12.7 us
    dot_general x10, matrix products, head_step(): spread = jnp.dot(g_head, v_head.T, preferred_element_type=jnp.float32)  11.6 us
  transfers between devices with their start and end apart: 3, of which 2 were waited for; matrix products, arithmetic and copies ran while one was open for 5% of the time, Pallas kernels for 0%

commit v1 on v0

v1 whole, which is shorter than its diff:
```python
import functools
import math

import jax
import jax.numpy as jnp
from jax import lax
from jax.experimental import pallas as pl
from jax.experimental.pallas import tpu as pltpu
from jax.sharding import PartitionSpec as P

MESH = pl.DeviceIdType.MESH
LOG2E = math.log2(math.e)
VMEM = pl.BlockSpec(memory_space=pltpu.VMEM)


def place(levels):
    me = lax.axis_index("tokens")
    bits = [(me // 2**k) % 2 for k in range(levels)]
    position = sum(bits[k] * 2 ** (levels - 1 - k) for k in range(levels))
    partners = []
    for s in range(levels):
        step = 2 ** (levels - 1 - s)
        partners.append(me + step - 2 * step * bits[levels - 1 - s])
    return position, partners


def greet(partners):
    barrier = pltpu.get_barrier_semaphore()
    for partner in partners:
        pl.semaphore_signal(barrier, inc=1, device_id={"tokens": partner}, device_id_type=MESH)
    pl.semaphore_wait(barrier, len(partners))


def gather_kernel(levels, rows_ref, stat_ref, rows_out, stat_out, send_sem, recv_sem, stat_send, stat_recv):
    position, partners = place(levels)
    chunks = rows_ref.shape[0]
    greet(partners)
    rows_out[position] = rows_ref[...]
    stat_out[position] = stat_ref[...]
    copies = {}
    for s in range(levels):
        size = 2**s
        start = position - position % size
        held = pl.ds(start, size)
        for c in range(chunks + 1):
            if s > 0:
                copies[s - 1, c].wait_recv()
            if c < chunks:
                view = rows_out.at[held, c]
                sems = (send_sem.at[s, c], recv_sem.at[s, c])
            else:
                view = stat_out.at[held]
                sems = (stat_send.at[s], stat_recv.at[s])
            copies[s, c] = pltpu.make_async_remote_copy(
                src_ref=view,
                dst_ref=view,
                send_sem=sems[0],
                recv_sem=sems[1],
                device_id={"tokens": partners[s]},
                device_id_type=MESH,
            )
            copies[s, c].start()
    for c in range(chunks + 1):
        copies[levels - 1, c].wait_recv()
    for copy in copies.values():
        copy.wait_send()


def gather_rows(count, rows, stats):
    levels = count.bit_length() - 1
    chunks = rows.shape[0]
    return pl.pallas_call(
        functools.partial(gather_kernel, levels),
        out_shape=(
            jax.ShapeDtypeStruct((count,) + rows.shape, rows.dtype),
            jax.ShapeDtypeStruct((count,) + stats.shape, stats.dtype),
        ),
        in_specs=[VMEM, VMEM],
        out_specs=(VMEM, VMEM),
        scratch_shapes=[
            pltpu.SemaphoreType.DMA((levels, chunks)),
            pltpu.SemaphoreType.DMA((levels, chunks)),
            pltpu.SemaphoreType.DMA((levels,)),
            pltpu.SemaphoreType.DMA((levels,)),
        ],
        compiler_params=pltpu.CompilerParams(
            collective_id=0, has_side_effects=True, vmem_limit_bytes=40 << 20
        ),
        name="gather_rows",
    )(rows, stats)


def head_kernel(lambda_ref, q_ref, g_ref, k_ref, v_ref, stat_ref, dq_ref, dk_ref, dv_ref, stat_t):
    head = pl.program_id(0)
    heads = pl.num_programs(0)
    me = lax.axis_index("tokens")
    blocks, _, block_rows, key_size = q_ref.shape
    rows = blocks * block_rows
    scale = float(key_size) ** -0.5

    @pl.when(head == 0)
    def _():
        stat_t[...] = stat_ref[...].reshape(rows, stat_ref.shape[2]).T

    def flat(x):
        return x.astype(jnp.float32).reshape(rows, x.shape[2]).astype(jnp.bfloat16)

    def row(i):
        return stat_t[pl.ds(i, 1), :]

    def dot(a, b, dims):
        return lax.dot_general(a, b, (dims, ((), ())), preferred_element_type=jnp.float32)

    weight_two = lambda_ref[head]
    live = row(4 * heads + me)
    g = flat(g_ref[:, 0])
    spread = dot(v_ref[...], g, ((1,), (1,)))
    probs = []
    for m in range(2):
        q = flat(q_ref[:, m])
        k = k_ref[m]
        score = dot(k, q, ((1,), (1,)))
        prob = live * jnp.exp2(score * (scale * LOG2E) - row(m * heads + head))
        coef_spread = spread if m == 0 else -weight_two * spread
        grad = (prob * (coef_spread - row((2 + m) * heads + head))).astype(jnp.bfloat16)
        probs.append(prob)
        dk_ref[m] = (dot(grad, q, ((1,), (0,))) * scale).astype(jnp.bfloat16)
        dq = dot(grad, k, ((0,), (0,))) * scale
        dq_ref[:, m] = dq.reshape(blocks, block_rows, key_size)
    mixed = (probs[0] - weight_two * probs[1]).astype(jnp.bfloat16)
    dv_ref[...] = dot(mixed, g, ((1,), (0,))).astype(jnp.bfloat16)


def heads_backward(rows, stats, keys, values, lambdas):
    heads = lambdas.shape[0]
    count, _, block_rows, width = rows.shape
    frames = keys.shape[1]
    key_size, value_size = width // heads, values.shape[1] // heads
    per_half = heads // 2
    return pl.pallas_call(
        head_kernel,
        out_shape=(
            jax.ShapeDtypeStruct((count, 2, block_rows, width), jnp.float32),
            jax.ShapeDtypeStruct(keys.shape, jnp.bfloat16),
            jax.ShapeDtypeStruct(values.shape, jnp.bfloat16),
        ),
        grid=(heads,),
        in_specs=[
            pl.BlockSpec(memory_space=pltpu.SMEM),
            pl.BlockSpec((count, 2, block_rows, key_size), lambda h: (0, 0, 0, h)),
            pl.BlockSpec((count, 1, block_rows, value_size), lambda h: (0, 2 + h // per_half, 0, h % per_half)),
            pl.BlockSpec((2, frames, key_size), lambda h: (0, 0, h)),
            pl.BlockSpec((frames, value_size), lambda h: (0, h)),
            pl.BlockSpec(stats.shape, lambda h: (0, 0, 0)),
        ],
        out_specs=(
            pl.BlockSpec((count, 2, block_rows, key_size), lambda h: (0, 0, 0, h)),
            pl.BlockSpec((2, frames, key_size), lambda h: (0, 0, h)),
            pl.BlockSpec((frames, value_size), lambda h: (0, h)),
        ),
        scratch_shapes=[pltpu.VMEM((stats.shape[2], count * block_rows), jnp.float32)],
        compiler_params=pltpu.CompilerParams(
            dimension_semantics=("arbitrary",), vmem_limit_bytes=48 << 20
        ),
        name="heads_backward",
    )(lambdas, rows, rows, keys, values, stats)


def sum_kernel(levels, chunks, part_ref, out_ref, total, sending, landed, send_sem, recv_sem):
    position, partners = place(levels)
    maps, width = part_ref.shape[1], part_ref.shape[3] // (chunks // part_ref.shape[1])
    per_map = chunks // maps
    greet(partners)
    copies = {}

    def cut(c):
        return (c // per_map, slice(None), slice((c % per_map) * width, (c % per_map + 1) * width))

    def send(s, c, source):
        size = 2**s
        bit = (position // size) % 2
        start = position - position % size + size - 2 * size * bit
        away = (pl.ds(start, size),) + cut(c)
        sending[away] = source[away].astype(sending.dtype)
        copies[s, c] = pltpu.make_async_remote_copy(
            src_ref=sending.at[away],
            dst_ref=landed.at[(pl.ds(size, size),) + cut(c)],
            send_sem=send_sem.at[s, c],
            recv_sem=recv_sem.at[s, c],
            device_id={"tokens": partners[s]},
            device_id_type=MESH,
        )
        copies[s, c].start()

    for c in range(chunks):
        send(levels - 1, c, part_ref)
    for s in range(levels - 1, -1, -1):
        size = 2**s
        source = part_ref if s == levels - 1 else total
        kept = pl.ds(position - position % size, size)
        for c in range(chunks):
            copies[s, c].wait_recv()
            got = landed[(pl.ds(size, size),) + cut(c)].astype(jnp.float32)
            new = source[(kept,) + cut(c)] + got
            if s > 0:
                total[(kept,) + cut(c)] = new
                send(s - 1, c, total)
            else:
                out_ref[cut(c)] = new[0].astype(out_ref.dtype)
    for copy in copies.values():
        copy.wait_send()


def sum_rows(part):
    count = part.shape[0]
    levels = count.bit_length() - 1
    chunks = 2 * part.shape[1]
    return pl.pallas_call(
        functools.partial(sum_kernel, levels, chunks),
        out_shape=jax.ShapeDtypeStruct(part.shape[1:], jnp.bfloat16),
        in_specs=[VMEM],
        out_specs=VMEM,
        scratch_shapes=[
            pltpu.VMEM(part.shape, jnp.float32),
            pltpu.VMEM(part.shape, jnp.bfloat16),
            pltpu.VMEM(part.shape, jnp.bfloat16),
            pltpu.SemaphoreType.DMA((levels, chunks)),
            pltpu.SemaphoreType.DMA((levels, chunks)),
        ],
        compiler_params=pltpu.CompilerParams(
            collective_id=1, has_side_effects=True, vmem_limit_bytes=40 << 20
        ),
        name="sum_rows",
    )(part)


def per_device(
    text_query, frame_key, frame_value, forward_out, out_grad, log_norms, lambdas, visits, bounds, text_count
):
    count = lax.axis_size("tokens")
    me = lax.axis_index("tokens")
    rows = text_query.shape[0]
    heads = lambdas.shape[0]
    value_size = frame_value.shape[1] // heads
    width = visits.shape[1] // 2

    grads = out_grad.astype(jnp.float32).reshape(rows, 1, heads, value_size)
    outs = forward_out.astype(jnp.float32).reshape(rows, 2, heads, value_size)
    coefs = jnp.stack([jnp.ones_like(lambdas), -lambdas])
    slopes = jnp.sum(grads * outs, axis=3) * coefs[None]
    mine = lax.dynamic_index_in_dim(visits, me, 0, keepdims=False)
    bound = lax.dynamic_index_in_dim(bounds, me, 0, keepdims=False)
    row_ids = jnp.arange(rows, dtype=jnp.int32)
    listed = jnp.where((row_ids >= bound)[:, None], mine[None, width:], mine[None, :width])
    hit = jnp.any(listed[:, :, None] == jnp.arange(count, dtype=jnp.int32)[None, None, :], axis=1)
    live = jnp.logical_and(hit, (me * rows + row_ids < text_count[0])[:, None]).astype(jnp.float32)
    lanes = -(-(4 * heads + count) // 128) * 128
    stats = jnp.concatenate(
        [
            log_norms.reshape(rows, 2 * heads) * LOG2E,
            slopes.reshape(rows, 2 * heads),
            live,
            jnp.zeros((rows, lanes - 4 * heads - count), jnp.float32),
        ],
        axis=1,
    )
    half = out_grad.shape[1] // 2
    sent = jnp.concatenate(
        [text_query.transpose(1, 0, 2), out_grad.reshape(rows, 2, half).transpose(1, 0, 2)], axis=0
    )
    all_rows, all_stats = gather_rows(count, sent, stats)
    part, key_grad, value_grad = heads_backward(
        all_rows, all_stats, frame_key.transpose(1, 0, 2), frame_value, lambdas
    )
    query_grad = sum_rows(part)
    return query_grad.transpose(1, 0, 2), key_grad.transpose(1, 0, 2), value_grad


def solution(mesh):
    both = ("groups", "tokens")
    return jax.shard_map(
        per_device,
        mesh=mesh,
        in_specs=(
            P(both, None, None),
            P(both, None, None),
            P(both, None),
            P(both, None, None),
            P(both, None),
            P(both, None, None),
            P(),
            P("groups", None),
            P("groups"),
            P(),
        ),
        out_specs=(P(both, None, None), P(both, None, None), P(both, None)),
        check_vma=False,
    )
```

time: 246 us -> 65 us (0.26); the launches traced: 243 us -> 64.3 us
  local copies, waits for them, and re-layouts: 74.1 us -> 12.6 us
  matrix products: 52.4 us -> 0 us
  Pallas kernels: 0 us -> 47.1 us
  blocking collectives: 43.8 us -> 0 us
  waiting for transfers between devices: 26.7 us -> 0 us
  other arithmetic: 19.5 us -> 3.23 us
  starting transfers between devices: 16.1 us -> 0 us
  loops' own time: 7.6 us -> 0 us
    dot_general x81 -> x0, matrix products: 52.4 us -> none  [the longest x10 28 us: head_step(): jnp.dot(mixed_weight.T, g_head, preferred_element_type=jnp.float32)]
    pallas_call x0 -> x3, Pallas kernels: none -> 47.1 us  [the longest x1 20.7 us: gather_rows(): pl.pallas_call(functools.partial(gather_kernel, levels), out_shape=(jax.S...]
    all_gather x2 -> x0, blocking collectives: 43.8 us -> none  [the longest x1 24.8 us: per_device(): lax.all_gather(log_norms, 'tokens', axis=0, tiled=True)]
    all_to_all x3 -> x0, waiting for transfers between devices: 26.7 us -> none  [the longest x1 13.8 us: per_device(): lax.all_to_all(query_part, 'tokens', split_axis=0, concat_axis=0, tiled=T...]
    dynamic_update_slice x20 -> x0, local copies, waits for them, and re-layouts: 20.1 us -> none  [the longest x10 12.7 us: head_step(): lax.dynamic_update_slice_in_dim(key_total, key_old + key_new, head_index...]
    slice x20 -> x0, local copies, waits for them, and re-layouts: 18.1 us -> none  [the longest x10 16.7 us: head_step(): k_head[:, 0]]
    dynamic_slice x22 -> x2, local copies, waits for them, and re-layouts: 18.6 us -> 1.26 us  [the longest x1 1.24 us: per_device(): bound = lax.dynamic_index_in_dim(bounds, me, 0, keepdims=False)]
    all_to_all x3 -> x0, starting transfers between devices: 16.1 us -> none  [the longest x1 7.39 us: per_device(): lax.all_to_all(sent_grad, 'tokens', split_axis=0, concat_axis=0, tiled=True)]
  transfers between devices with their start and end apart: 3 -> 0, of which waited for: 2 -> 0; matrix products, arithmetic and copies ran while one was open for 5% -> 0% of each run, Pallas kernels for 0% -> 0%
where the time goes in v1:
time: 65 us; the launch traced here: 64.3 us
  Pallas kernels  47.1 us (72%)
  local copies, waits for them, and re-layouts  12.6 us (19%)
  other arithmetic  3.23 us (5%)
  between operations  1.39 us (2%)
    pallas_call x1, Pallas kernels, gather_rows(): pl.pallas_call(functools.partial(gather_kernel, levels), out_shape=(jax.S...  20.7 us
    pallas_call x1, Pallas kernels, sum_rows(): pl.pallas_call(functools.partial(sum_kernel, levels, chunks), out_shape=j...  14.3 us
    pallas_call x1, Pallas kernels, heads_backward(): pl.pallas_call(head_kernel, out_shape=(jax.ShapeDtypeStruct((count, 2, bl...  12 us
    unnamed x8, local copies, waits for them, and re-layouts  9.19 us

profile of v1, /device:TPU:0, one launch (start us, length us, event | category | flops | bytes accessed | tf_op | source)
XLA Modules:
  0.0 64.3 jit_solution(1213072500866905182)
XLA Ops:
  0.6 0.0 copy-start
  1.3 1.2 %dynamic_slice.8 = s32[1]{0:T(128)} dynamic-slice(s32[16]{0:T(128)} %param.18, s32[]{:T(128)S(6)} %select_n.14), dynamic_slice_sizes={1} | dynamic-slice | bytes 12 | tf_op jit(solution)/shard_map/jit(dynamic_index_in_dim)/dynamic_slice | solution.py:252
  2.6 0.6 %iota_compare_fusion.1 = pred[8]{0:T(512)(128)(4,1)S(1)} fusion(s32[]{:T(128)} %bitcast.5), kind=kLoop, calls=%fused_computation.14 | loop fusion | flops 8 | bytes 12 | tf_op jit(solution)/shard_map/ge | solution.py:254
  3.2 0.0 copy-done
  3.2 0.7 %negate_bitcast_fusion = f32[1,10]{1,0:T(1,128)S(1)} fusion(f32[10]{0:T(128)} %lambda_ref.1), kind=kLoop, calls=%fused_computation.15 | loop fusion | flops 10 | bytes 80 | tf_op jit(solution)/shard_map/stack | solution.py:249
  3.9 0.1 mul.43
  4.0 0.1 pad.4.clone
  4.1 0.1 slice_bitcast_fusion.1
  4.2 0.1 broadcast_select_fusion
  4.2 0.1 fusion
  4.3 0.1 and_convert_fusion
  4.4 0.7 %broadcast_multiply_fusion = f32[8,2,10]{2,1,0:T(2,128)S(1)} fusion(f32[8,2,10]{2,1,0:T(2,128)} %param.15), kind=kLoop, calls=%fused_computation.7 | loop fusion | flops 160 | bytes 1280 | tf_op jit(solution)/shard_map/mul | solution.py:260
  5.1 0.1 mul.38
  5.2 0.8 %copy.41 = bf16[8,2,1280]{2,0,1:T(8,128)(2,1)S(1)} copy(bf16[8,2,1280]{2,1,0:T(2,128)(2,1)} %param.10) | data formatting | bytes 81920 | tf_op args[0]
  6.0 0.8 %pad_maximum_fusion.rows_ref = bf16[4,8,1280]{2,1,0:T(8,128)(2,1)S(1)} fusion(bf16[2,8,1280]{2,1,0:T(8,128)(2,1)} %bitcast.28, bf16[2,8,1280]{2,1,0:T(8,128)(2,1)S(1)} %bitcast.27), kind=kLoop, calls=%fused_computation.2 | loop fusion | flops 40960 | bytes 163840 | tf_op jit(solution)/shard_map/concatenate | solution.py:268
  6.7 0.8 %copy.32 = f32[8,10,256]{2,1,0:T(8,128)S(1)} copy(bf16[8,10,256]{2,0,1:T(8,128)(2,1)} %bitcast.29) | data formatting | bytes 122880 | tf_op jit(solution)/shard_map/mul | solution.py:250
  7.5 0.9 %copy.33 = f32[8,2,2560]{2,0,1:T(8,128)S(1)} copy(bf16[8,2,2560]{2,1,0:T(2,128)(2,1)} %param.13) | data formatting | bytes 245760 | tf_op jit(solution)/shard_map/reshape | solution.py:248
  8.5 0.1 multiply_reduce_fusion
  8.6 0.1 reduce_sum.12
  8.7 0.1 maximum_maximum_fusion.stat_ref
  8.8 20.7 %gather_rows.1 = (bf16[16,4,8,1280]{3,2,1,0:T(8,128)(2,1)S(1)}, f32[16,8,128]{2,1,0:T(8,128)S(1)}) custom-call(bf16[4,8,1280]{2,1,0:T(8,128)(2,1)S(1)} %pad_maximum_fusion.rows_ref, f32[8,128]{1,0:T(8,128)S(1)} %maximum_maximum_fusion.stat_ref), custom_call_target="tpu_custom_call" | custom-call | tf_op jit(solution)/shard_map/gather_rows/pallas_call | solution.py:72
  29.5 0.0 copy-start.1
  29.5 3.6 %copy.40 = bf16[512,2,1280]{2,0,1:T(8,128)(2,1)} copy(bf16[512,2,1280]{2,1,0:T(2,128)(2,1)} %param.11) | data formatting | bytes 5242880 | tf_op args[1]
  33.1 0.0 copy-done.1
  33.1 12.0 %heads_backward.1 = (f32[16,2,8,1280]{3,2,1,0:T(8,128)S(1)}, bf16[2,512,1280]{2,1,0:T(8,128)(2,1)S(1)}, bf16[512,2560]{1,0:T(8,128)(2,1)}) custom-call(f32[10]{0:T(128)S(1)} %copy-done.1, bf16[16,4,8,1280]{3,2,1,0:T(8,128)(2,1)S(1)} %get-tuple-element.8.q_ref.g_ref, bf16[16,4,8,1280]{3,2,1,0:T(8,128)(2,1)S(1)} %get-tuple-element.8.q_ref.g_ref, ...), custom_call_target="tpu_custom_call" | custom-call | tf_op jit(solution)/shard_map/heads_backward/pallas_call | solution.py:140
  45.1 14.3 %sum_rows.1 = bf16[2,8,1280]{2,1,0:T(8,128)(2,1)S(1)} custom-call(f32[16,2,8,1280]{3,2,1,0:T(8,128)S(1)} %get-tuple-element.10.part_ref), custom_call_target="tpu_custom_call" | custom-call | tf_op jit(solution)/shard_map/sum_rows/pallas_call | solution.py:218
  59.5 0.6 %copy.36 = bf16[8,2,1280]{2,1,0:T(2,128)(2,1)} copy(bf16[8,2,1280]{2,0,1:T(8,128)(2,1)S(1)} %bitcast.25) | data formatting | bytes 81920
  60.1 4.2 %copy.37 = bf16[512,2,1280]{2,1,0:T(2,128)(2,1)} copy(bf16[512,2,1280]{2,0,1:T(8,128)(2,1)S(1)} %bitcast.24) | data formatting | bytes 5242880
  (7 shorter events, 0.1 us)
Async XLA Ops:
  0.6 2.6 %copy-start = (s32[16,12]{1,0:T(8,128)S(1)}, s32[16,12]{1,0:T(8,128)}, u32[]{:S(2)}) copy-start(s32[16,12]{1,0:T(8,128)} %param.17) | copy-start | bytes 2308
  29.5 3.6 %copy-start.1 = (f32[10]{0:T(128)S(1)}, f32[10]{0:T(128)}, u32[]{:S(2)}) copy-start(f32[10]{0:T(128)} %lambda_ref.1) | copy-start | bytes 124

commit v2 on v1

v2 whole, which is shorter than its diff:
```python
import functools
import math

import jax
import jax.numpy as jnp
from jax import lax
from jax.experimental import pallas as pl
from jax.experimental.pallas import tpu as pltpu
from jax.sharding import PartitionSpec as P

MESH = pl.DeviceIdType.MESH
LOG2E = math.log2(math.e)
VMEM = pl.BlockSpec(memory_space=pltpu.VMEM)


def place(levels):
    me = lax.axis_index("tokens")
    bits = [(me // 2**k) % 2 for k in range(levels)]
    position = sum(bits[k] * 2 ** (levels - 1 - k) for k in range(levels))
    partners = []
    for s in range(levels):
        step = 2 ** (levels - 1 - s)
        partners.append(me + step - 2 * step * bits[levels - 1 - s])
    return position, partners


def greet(partners):
    barrier = pltpu.get_barrier_semaphore()
    for partner in partners:
        pl.semaphore_signal(barrier, inc=1, device_id={"tokens": partner}, device_id_type=MESH)
    pl.semaphore_wait(barrier, len(partners))


def fused_kernel(
    levels,
    heads,
    lag,
    lambda_ref,
    visit_ref,
    bound_ref,
    count_ref,
    norm_ref,
    q_in,
    g_in,
    o_in,
    k_ref,
    v_ref,
    out_ref,
    dk_ref,
    dv_ref,
    rows_all,
    stat_all,
    stat_t,
    total,
    sending,
    landed,
    gather_send,
    gather_recv,
    stat_send,
    stat_recv,
    sum_send,
    sum_recv,
):
    step = pl.program_id(0)
    me = lax.axis_index("tokens")
    position, partners = place(levels)
    block_rows, key_size, value_size = q_in.shape[1], k_ref.shape[2], v_ref.shape[1]
    count = rows_all.shape[1]
    rows = count * block_rows
    scale = float(key_size) ** -0.5
    last = levels - 1
    warm = lag * levels

    def held(s):
        return pl.ds(position - position % 2**s, 2**s)

    def other(s):
        size = 2**s
        return pl.ds(position - position % size + size - 2 * size * ((position // size) % 2), size)

    def remote(s, source, target, send, recv):
        return pltpu.make_async_remote_copy(
            src_ref=source,
            dst_ref=target,
            send_sem=send,
            recv_sem=recv,
            device_id={"tokens": partners[s]},
            device_id_type=MESH,
        )

    def gather_copy(s, h, where):
        view = rows_all.at[h, where(s)]
        return remote(s, view, view, gather_send.at[s, h], gather_recv.at[s, h])

    def stat_copy(s, where):
        view = stat_all.at[where(s)]
        return remote(s, view, view, stat_send.at[s], stat_recv.at[s])

    def sum_copy(s, h):
        return remote(
            s, sending.at[h, other(s)], landed.at[h, pl.ds(2**s, 2**s)], sum_send.at[s, h], sum_recv.at[s, h]
        )

    @pl.when(step == 0)
    def _():
        greet(partners)
        for h in range(heads):
            keys = slice(h * key_size, (h + 1) * key_size)
            rows_all[h, position, :, 0:key_size] = q_in[0, :, keys]
            rows_all[h, position, :, key_size : 2 * key_size] = q_in[1, :, keys]
            rows_all[h, position, :, 2 * key_size :] = g_in[:, h * value_size : (h + 1) * value_size]
        lanes = lax.broadcasted_iota(jnp.int32, (block_rows, stat_all.shape[2]), 1)
        row_ids = lax.broadcasted_iota(jnp.int32, (block_rows, stat_all.shape[2]), 0)
        second = row_ids >= bound_ref[me]
        present = me * block_rows + row_ids < count_ref[0]
        width = visit_ref.shape[1] // 2
        stats = jnp.zeros((block_rows, stat_all.shape[2]), jnp.float32)
        for k in range(width):
            shard = jnp.where(second, visit_ref[me, width + k], visit_ref[me, k])
            stats = jnp.where(jnp.logical_and(lanes == 4 * heads + shard, present), 1.0, stats)
        stats = stats + norm_ref[...] * LOG2E
        for h in range(heads):
            values = slice(h * value_size, (h + 1) * value_size)
            g = g_in[:, values].astype(jnp.float32)
            for m in range(2):
                coef = 1.0 if m == 0 else -lambda_ref[h]
                slope = jnp.sum(g * o_in[m, :, values].astype(jnp.float32), axis=1, keepdims=True) * coef
                stats = jnp.where(lanes == (2 + m) * heads + h, slope, stats)
        stat_all[position] = stats

    for s in range(levels):
        h = step - lag * s

        @pl.when(jnp.logical_and(h >= 0, h < heads))
        def _():
            if s > 0:
                gather_copy(s - 1, h, other).wait_recv()
            gather_copy(s, h, held).start()

        @pl.when(h == 0)
        def _():
            if s > 0:
                stat_copy(s - 1, other).wait_recv()
            stat_copy(s, held).start()

    for s in range(last, -1, -1):
        h = step - warm - lag * (levels - s)

        @pl.when(jnp.logical_and(h >= 0, h < heads))
        def _():
            sum_copy(s, h).wait_recv()
            new = total[h, held(s)] + landed[h, pl.ds(2**s, 2**s)].astype(jnp.float32)
            if s > 0:
                total[h, held(s)] = new
                sending[h, other(s - 1)] = total[h, other(s - 1)].astype(sending.dtype)
                sum_copy(s - 1, h).start()
            else:
                out_ref[:, :, pl.ds(pl.multiple_of(h * key_size, key_size), key_size)] = new[0].astype(out_ref.dtype)

    head = step - warm

    @pl.when(head == 0)
    def _():
        stat_copy(last, other).wait_recv()
        stat_t[...] = stat_all[...].reshape(rows, stat_all.shape[2]).T

    @pl.when(jnp.logical_and(head >= 0, head < heads))
    def _():
        gather_copy(last, head, other).wait_recv()

        def flat(x):
            return x.astype(jnp.float32).reshape(rows, x.shape[2]).astype(jnp.bfloat16)

        def row(i):
            return stat_t[pl.ds(i, 1), :]

        def dot(a, b, dims):
            return lax.dot_general(a, b, (dims, ((), ())), preferred_element_type=jnp.float32)

        weight_two = lambda_ref[head]
        live = row(4 * heads + me)
        g = flat(rows_all[head, :, :, 2 * key_size :])
        spread = dot(v_ref[...], g, ((1,), (1,)))
        probs = []
        for m in range(2):
            q = flat(rows_all[head, :, :, m * key_size : (m + 1) * key_size])
            k = k_ref[m]
            score = dot(k, q, ((1,), (1,)))
            prob = live * jnp.exp2(score * (scale * LOG2E) - row(m * heads + head))
            coef_spread = spread if m == 0 else -weight_two * spread
            grad = (prob * (coef_spread - row((2 + m) * heads + head))).astype(jnp.bfloat16)
            probs.append(prob)
            dq = dot(grad, k, ((0,), (0,))) * scale
            total[head, :, m] = dq.reshape(count, block_rows, key_size)
            dk_ref[m] = (dot(grad, q, ((1,), (0,))) * scale).astype(jnp.bfloat16)
        sending[head, other(last)] = total[head, other(last)].astype(sending.dtype)
        sum_copy(last, head).start()
        mixed = (probs[0] - weight_two * probs[1]).astype(jnp.bfloat16)
        dv_ref[...] = dot(mixed, g, ((1,), (0,))).astype(jnp.bfloat16)

    @pl.when(step == pl.num_programs(0) - 1)
    def _():
        for s in range(levels):
            stat_copy(s, held).wait_send()

            @pl.loop(0, heads)
            def _(h):
                gather_copy(s, h, held).wait_send()
                sum_copy(s, h).wait_send()


def per_device(
    text_query, frame_key, frame_value, forward_out, out_grad, log_norms, lambdas, visits, bounds, text_count
):
    count = lax.axis_size("tokens")
    levels = count.bit_length() - 1
    lag = 1
    block_rows = text_query.shape[0]
    heads = lambdas.shape[0]
    frames = frame_key.shape[0]
    key_size, value_size = text_query.shape[2] // heads, frame_value.shape[1] // heads
    lanes = -(-(4 * heads + count) // 128) * 128
    norms = jnp.pad(log_norms.reshape(block_rows, 2 * heads), ((0, 0), (0, lanes - 2 * heads)))
    warm = lag * levels
    dma = pltpu.SemaphoreType.DMA
    smem = pl.BlockSpec(memory_space=pltpu.SMEM)

    def whole(shape):
        return pl.BlockSpec(shape, lambda j: (0,) * len(shape))

    def at(j):
        return jnp.clip(j - warm, 0, heads - 1)

    key_spec = pl.BlockSpec((2, frames, key_size), lambda j: (0, 0, at(j)))
    value_spec = pl.BlockSpec((frames, value_size), lambda j: (0, at(j)))
    queries = text_query.transpose(1, 0, 2)
    keys = frame_key.transpose(1, 0, 2)
    outs = forward_out.transpose(1, 0, 2)
    query_grad, key_grad, value_grad = pl.pallas_call(
        functools.partial(fused_kernel, levels, heads, lag),
        out_shape=(
            jax.ShapeDtypeStruct(queries.shape, jnp.bfloat16),
            jax.ShapeDtypeStruct(keys.shape, jnp.bfloat16),
            jax.ShapeDtypeStruct(frame_value.shape, jnp.bfloat16),
        ),
        grid=(heads + 2 * warm,),
        in_specs=[
            smem,
            smem,
            smem,
            smem,
            whole(norms.shape),
            whole(queries.shape),
            whole(out_grad.shape),
            whole(outs.shape),
            key_spec,
            value_spec,
        ],
        out_specs=(whole(queries.shape), key_spec, value_spec),
        scratch_shapes=[
            pltpu.VMEM((heads, count, block_rows, 2 * key_size + value_size), jnp.bfloat16),
            pltpu.VMEM((count, block_rows, lanes), jnp.float32),
            pltpu.VMEM((lanes, count * block_rows), jnp.float32),
            pltpu.VMEM((heads, count, 2, block_rows, key_size), jnp.float32),
            pltpu.VMEM((heads, count, 2, block_rows, key_size), jnp.bfloat16),
            pltpu.VMEM((heads, count, 2, block_rows, key_size), jnp.bfloat16),
            dma((levels, heads)),
            dma((levels, heads)),
            dma((levels,)),
            dma((levels,)),
            dma((levels, heads)),
            dma((levels, heads)),
        ],
        compiler_params=pltpu.CompilerParams(
            dimension_semantics=("arbitrary",),
            collective_id=0,
            has_side_effects=True,
            vmem_limit_bytes=48 << 20,
        ),
        name="fused_backward",
    )(lambdas, visits, bounds, text_count, norms, queries, out_grad, outs, keys, frame_value)
    return query_grad.transpose(1, 0, 2), key_grad.transpose(1, 0, 2), value_grad


def solution(mesh):
    both = ("groups", "tokens")
    return jax.shard_map(
        per_device,
        mesh=mesh,
        in_specs=(
            P(both, None, None),
            P(both, None, None),
            P(both, None),
            P(both, None, None),
            P(both, None),
            P(both, None, None),
            P(),
            P("groups", None),
            P("groups"),
            P(),
        ),
        out_specs=(P(both, None, None), P(both, None, None), P(both, None)),
        check_vma=False,
    )
```

time: 65 us -> 66.1 us (1.017)
  Pallas kernels: 47.1 us -> 52.1 us
  other arithmetic: 3.23 us -> 0 us
    pallas_call x3 -> x1, Pallas kernels: 47.1 us -> 52.1 us  [per_device(): pl.pallas_call(functools.partial(fused_kernel, levels, heads, lag), out_s...]
    unnamed x8 -> x14, local copies, waits for them, and re-layouts: 9.19 us -> 11.6 us
    dynamic_slice x2 -> x0, local copies, waits for them, and re-layouts: 1.26 us -> none  [the longest x1 1.24 us: per_device(): bound = lax.dynamic_index_in_dim(bounds, me, 0, keepdims=False)]
    mul x3 -> x0, local copies, waits for them, and re-layouts: 0.96 us -> none  [the longest x2 0.87 us: per_device(): slopes = jnp.sum(grads * outs, axis=3) * coefs[None]]
    concatenate x2 -> x0, other arithmetic: 0.87 us -> none  [the longest x1 0.79 us: per_device(): jnp.concatenate([text_query.transpose(1, 0, 2), out_grad.reshape(rows, 2,...]
    mul x2 -> x0, other arithmetic: 0.71 us -> none  [the longest x1 0.71 us: per_device(): log_norms.reshape(rows, 2 * heads) * LOG2E]
where the time goes in v2:
time: 66.1 us; the launch traced here: 65.8 us
  Pallas kernels  52.1 us (79%)
  local copies, waits for them, and re-layouts  12.4 us (19%)
  between operations  1.34 us (2%)
    pallas_call x1, Pallas kernels, per_device(): pl.pallas_call(functools.partial(fused_kernel, levels, heads, lag), out_s...  52.1 us
    unnamed x14, local copies, waits for them, and re-layouts  11.6 us

profile of v2, /device:TPU:0, one launch (start us, length us, event | category | flops | bytes accessed | tf_op | source)
XLA Modules:
  0.0 65.8 jit_solution(14659163606339772089)
XLA Ops:
  1.3 0.8 %reshape.9 = f32[8,20]{1,0:T(8,128)S(1)} reshape(f32[8,2,10]{2,1,0:T(2,128)} %param.15) | data formatting | bytes 1280 | tf_op jit(solution)/shard_map/reshape | solution.py:223
  2.1 0.8 %copy.23 = bf16[8,2,1280]{2,0,1:T(8,128)(2,1)S(1)} copy(bf16[8,2,1280]{2,1,0:T(2,128)(2,1)} %param.10) | data formatting | bytes 81920 | tf_op args[0]
  2.8 0.9 %copy.22 = bf16[8,2,2560]{2,0,1:T(8,128)(2,1)S(1)} copy(bf16[8,2,2560]{2,1,0:T(2,128)(2,1)} %param.13) | data formatting | bytes 163840 | tf_op args[3]
  3.7 0.0 copy-start
  3.8 0.0 copy-start.1
  3.8 0.0 copy-start.2
  3.8 0.0 copy-start.3
  3.8 3.6 %copy.21 = bf16[512,2,1280]{2,0,1:T(8,128)(2,1)} copy(bf16[512,2,1280]{2,1,0:T(2,128)(2,1)} %param.11) | data formatting | bytes 5242880 | tf_op args[1]
  7.4 0.0 copy-done
  7.4 0.0 copy-done.1
  7.4 0.0 copy-done.2
  7.4 0.0 copy-done.3
  7.4 52.1 %fused_backward.1 = (bf16[2,8,1280]{2,1,0:T(8,128)(2,1)S(1)}, bf16[2,512,1280]{2,1,0:T(8,128)(2,1)S(1)}, bf16[512,2560]{1,0:T(8,128)(2,1)S(1)}) custom-call(f32[10]{0:T(128)S(1)} %copy-done.2, s32[16,12]{1,0:T(8,128)S(1)} %copy-done.1, s32[16]{0:T(128)S(1)} %copy-done.3, s32[1]{0:T(128)S(6)} %copy.25.count_ref, f32[8,128]{1,0:T(8,128)S(1)} %pad.4.norm_ref, ...), custom_call_target="tpu_custom_call" | custom-call | tf_op jit(solution)/shard_map/fused_backward/pallas_call | solution.py:239
  59.5 0.6 copy.16
  60.1 4.2 %copy.17 = bf16[512,2,1280]{2,1,0:T(2,128)(2,1)} copy(bf16[512,2,1280]{2,0,1:T(8,128)(2,1)S(1)} %bitcast.11) | data formatting | bytes 5242880
  64.3 1.5 %copy.26 = bf16[512,2560]{1,0:T(8,128)(2,1)} copy(bf16[512,2560]{1,0:T(8,128)(2,1)S(1)} %get-tuple-element.17) | data formatting | bytes 5242880
  (1 shorter events, 0.0 us)
Async XLA Ops:
  3.7 3.6 %copy-start = (bf16[8,2560]{1,0:T(8,128)(2,1)S(1)}, bf16[8,2560]{1,0:T(8,128)(2,1)}, u32[]{:S(2)}) copy-start(bf16[8,2560]{1,0:T(8,128)(2,1)} %g_in.1) | copy-start | bytes 122884
  3.8 3.6 %copy-start.1 = (s32[16,12]{1,0:T(8,128)S(1)}, s32[16,12]{1,0:T(8,128)}, u32[]{:S(2)}) copy-start(s32[16,12]{1,0:T(8,128)} %visit_ref.1) | copy-start | bytes 2308
  3.8 3.6 %copy-start.2 = (f32[10]{0:T(128)S(1)}, f32[10]{0:T(128)}, u32[]{:S(2)}) copy-start(f32[10]{0:T(128)} %lambda_ref.1) | copy-start | bytes 124
  3.8 3.6 %copy-start.3 = (s32[16]{0:T(128)S(1)}, s32[16]{0:T(128)}, u32[]{:S(2)}) copy-start(s32[16]{0:T(128)} %bound_ref.1) | copy-start | bytes 196

commit v3 on v2

v3 whole, which is shorter than its diff:
```python
import functools
import math

import jax
import jax.numpy as jnp
from jax import lax
from jax.experimental import pallas as pl
from jax.experimental.pallas import tpu as pltpu
from jax.sharding import PartitionSpec as P

MESH = pl.DeviceIdType.MESH
LOG2E = math.log2(math.e)
VMEM = pl.BlockSpec(memory_space=pltpu.VMEM)


def radices_of(count):
    radices, left = [], count
    while left > 1:
        radix = 2 if len(radices) < 2 or left % 4 else 4
        radices.append(radix)
        left //= radix
    return tuple(reversed(radices))


def place(radices):
    me = lax.axis_index("tokens")
    stride = math.prod(radices)
    position, weight, digits, partners = 0, 1, [], []
    for radix in radices:
        stride //= radix
        digit = (me // stride) % radix
        digits.append(digit)
        partners.append([me + ((digit + r) % radix - digit) * stride for r in range(1, radix)])
        position = position + digit * weight
        weight *= radix
    return position, digits, partners


def greet(partners):
    barrier = pltpu.get_barrier_semaphore()
    partners = [p for group in partners for p in group]
    for partner in partners:
        pl.semaphore_signal(barrier, inc=1, device_id={"tokens": partner}, device_id_type=MESH)
    pl.semaphore_wait(barrier, len(partners))


def fused_kernel(
    radices,
    heads,
    chunks,
    lag,
    lambda_ref,
    visit_ref,
    bound_ref,
    count_ref,
    norm_ref,
    q_in,
    g_in,
    o_in,
    k_ref,
    v_ref,
    out_ref,
    dk_ref,
    dv_ref,
    rows_all,
    stat_all,
    stat_t,
    total,
    sending,
    landed,
    gather_send,
    gather_recv,
    stat_send,
    stat_recv,
    sum_send,
    sum_recv,
):
    step = pl.program_id(0)
    me = lax.axis_index("tokens")
    levels = len(radices)
    sizes = [math.prod(radices[:s]) for s in range(levels)]
    position, digits, partners = place(radices)
    per = heads // chunks
    block_rows, key_size, value_size = q_in.shape[1], k_ref.shape[2] // per, v_ref.shape[1] // per
    key_wide, value_wide = per * key_size, per * value_size
    count = rows_all.shape[1]
    rows = count * block_rows
    scale = float(key_size) ** -0.5
    last = levels - 1
    warm = lag * levels

    def held(s):
        return pl.ds(position - position % sizes[s], sizes[s])

    def part(s, r):
        size, radix = sizes[s], radices[s]
        return pl.ds(position - position % (size * radix) + (digits[s] + r + radix) % radix * size, size)

    def slot(s, r):
        return pl.ds(r * sizes[s], sizes[s])

    def hops(s):
        return range(1, radices[s])

    def remote(s, r, source, target, send, recv):
        return pltpu.make_async_remote_copy(
            src_ref=source,
            dst_ref=target,
            send_sem=send,
            recv_sem=recv,
            device_id={"tokens": partners[s][r - 1]},
            device_id_type=MESH,
        )

    def gather_copy(s, h, r, where):
        view = rows_all.at[h, where]
        return remote(s, r, view, view, gather_send.at[s, r, h], gather_recv.at[s, r, h])

    def stat_copy(s, r, where):
        view = stat_all.at[where]
        return remote(s, r, view, view, stat_send.at[s, r], stat_recv.at[s, r])

    def sum_copy(s, h, r):
        return remote(
            s, r, sending.at[h, part(s, r)], landed.at[h, slot(s, r)], sum_send.at[s, r, h], sum_recv.at[s, r, h]
        )

    def gather_arrived(s, h):
        for r in hops(s):
            gather_copy(s, h, r, part(s, -r)).wait_recv()

    def stats_arrived(s):
        for r in hops(s):
            stat_copy(s, r, part(s, -r)).wait_recv()

    def send_sums(s, h):
        for r in hops(s):
            away = part(s, r)
            sending[h, away] = total[h, away].astype(sending.dtype)
            sum_copy(s, h, r).start()

    @pl.when(step == 0)
    def _():
        greet(partners)
        for c in range(chunks):
            keys = slice(c * key_wide, (c + 1) * key_wide)
            rows_all[c, position, :, 0:key_wide] = q_in[0, :, keys]
            rows_all[c, position, :, key_wide : 2 * key_wide] = q_in[1, :, keys]
            rows_all[c, position, :, 2 * key_wide :] = g_in[:, c * value_wide : (c + 1) * value_wide]
        lanes = lax.broadcasted_iota(jnp.int32, (block_rows, stat_all.shape[2]), 1)
        row_ids = lax.broadcasted_iota(jnp.int32, (block_rows, stat_all.shape[2]), 0)
        second = row_ids >= bound_ref[me]
        present = me * block_rows + row_ids < count_ref[0]
        width = visit_ref.shape[1] // 2
        stats = jnp.zeros((block_rows, stat_all.shape[2]), jnp.float32)
        for k in range(width):
            shard = jnp.where(second, visit_ref[me, width + k], visit_ref[me, k])
            stats = jnp.where(jnp.logical_and(lanes == 4 * heads + shard, present), 1.0, stats)
        stats = stats + norm_ref[...] * LOG2E
        for h in range(heads):
            values = slice(h * value_size, (h + 1) * value_size)
            g = g_in[:, values].astype(jnp.float32)
            for m in range(2):
                coef = 1.0 if m == 0 else -lambda_ref[h]
                slope = jnp.sum(g * o_in[m, :, values].astype(jnp.float32), axis=1, keepdims=True) * coef
                stats = jnp.where(lanes == (2 + m) * heads + h, slope, stats)
        stat_all[position] = stats

    for s in range(levels):
        h = step - lag * s

        @pl.when(jnp.logical_and(h >= 0, h < chunks))
        def _():
            if s > 0:
                gather_arrived(s - 1, h)
            for r in hops(s):
                gather_copy(s, h, r, held(s)).start()

        @pl.when(h == 0)
        def _():
            if s > 0:
                stats_arrived(s - 1)
            for r in hops(s):
                stat_copy(s, r, held(s)).start()

    for s in range(last, -1, -1):
        h = step - warm - lag * (levels - s)

        @pl.when(jnp.logical_and(h >= 0, h < chunks))
        def _():
            new = total[h, held(s)]
            for r in hops(s):
                sum_copy(s, h, r).wait_recv()
                new = new + landed[h, slot(s, r)].astype(jnp.float32)
            if s > 0:
                total[h, held(s)] = new
                send_sums(s - 1, h)
            else:
                out_ref[:, :, pl.ds(pl.multiple_of(h * key_wide, key_wide), key_wide)] = new[0].astype(out_ref.dtype)

    chunk = step - warm

    @pl.when(chunk == 0)
    def _():
        stats_arrived(last)
        stat_t[...] = stat_all[...].reshape(rows, stat_all.shape[2]).T

    @pl.when(jnp.logical_and(chunk >= 0, chunk < chunks))
    def _():
        gather_arrived(last, chunk)

        def flat(x):
            return x.astype(jnp.float32).reshape(rows, x.shape[2]).astype(jnp.bfloat16)

        def row(i):
            return stat_t[pl.ds(i, 1), :]

        def dot(a, b, dims):
            return lax.dot_general(a, b, (dims, ((), ())), preferred_element_type=jnp.float32)

        live = row(4 * heads + me)
        for i in range(per):
            head = chunk * per + i
            weight_two = lambda_ref[head]
            keys = slice(i * key_size, (i + 1) * key_size)
            values = slice(i * value_size, (i + 1) * value_size)
            g = flat(rows_all[chunk, :, :, 2 * key_wide + i * value_size : 2 * key_wide + (i + 1) * value_size])
            spread = dot(v_ref[:, values], g, ((1,), (1,)))
            probs = []
            for m in range(2):
                first = m * key_wide + i * key_size
                q = flat(rows_all[chunk, :, :, first : first + key_size])
                k = k_ref[m, :, keys]
                score = dot(k, q, ((1,), (1,)))
                prob = live * jnp.exp2(score * (scale * LOG2E) - row(m * heads + head))
                coef_spread = spread if m == 0 else -weight_two * spread
                grad = (prob * (coef_spread - row((2 + m) * heads + head))).astype(jnp.bfloat16)
                probs.append(prob)
                dq = dot(grad, k, ((0,), (0,))) * scale
                total[chunk, :, m, :, keys] = dq.reshape(count, block_rows, key_size)
                dk_ref[m, :, keys] = (dot(grad, q, ((1,), (0,))) * scale).astype(jnp.bfloat16)
            mixed = (probs[0] - weight_two * probs[1]).astype(jnp.bfloat16)
            dv_ref[:, values] = dot(mixed, g, ((1,), (0,))).astype(jnp.bfloat16)
        send_sums(last, chunk)

    @pl.when(step == pl.num_programs(0) - 1)
    def _():
        for s in range(levels):
            for r in hops(s):
                stat_copy(s, r, held(s)).wait_send()

                @pl.loop(0, chunks)
                def _(h):
                    gather_copy(s, h, r, held(s)).wait_send()
                    sum_copy(s, h, r).wait_send()


def per_device(
    text_query, frame_key, frame_value, forward_out, out_grad, log_norms, lambdas, visits, bounds, text_count
):
    count = lax.axis_size("tokens")
    radices = radices_of(count)
    levels, widest = len(radices), max(radices)
    lag = 1
    block_rows = text_query.shape[0]
    heads = lambdas.shape[0]
    chunks = heads // 2 if heads % 2 == 0 else heads
    frames = frame_key.shape[0]
    key_size, value_size = text_query.shape[2] // heads, frame_value.shape[1] // heads
    key_wide, value_wide = key_size * heads // chunks, value_size * heads // chunks
    lanes = -(-(4 * heads + count) // 128) * 128
    norms = jnp.pad(log_norms.reshape(block_rows, 2 * heads), ((0, 0), (0, lanes - 2 * heads)))
    warm = lag * levels
    dma = pltpu.SemaphoreType.DMA
    smem = pl.BlockSpec(memory_space=pltpu.SMEM)

    def whole(shape):
        return pl.BlockSpec(shape, lambda j: (0,) * len(shape))

    def at(j):
        return jnp.clip(j - warm, 0, chunks - 1)

    key_spec = pl.BlockSpec((2, frames, key_wide), lambda j: (0, 0, at(j)))
    value_spec = pl.BlockSpec((frames, value_wide), lambda j: (0, at(j)))
    queries = text_query.transpose(1, 0, 2)
    keys = frame_key.transpose(1, 0, 2)
    outs = forward_out.transpose(1, 0, 2)
    query_grad, key_grad, value_grad = pl.pallas_call(
        functools.partial(fused_kernel, radices, heads, chunks, lag),
        out_shape=(
            jax.ShapeDtypeStruct(queries.shape, jnp.bfloat16),
            jax.ShapeDtypeStruct(keys.shape, jnp.bfloat16),
            jax.ShapeDtypeStruct(frame_value.shape, jnp.bfloat16),
        ),
        grid=(chunks + 2 * warm,),
        in_specs=[
            smem,
            smem,
            smem,
            smem,
            whole(norms.shape),
            whole(queries.shape),
            whole(out_grad.shape),
            whole(outs.shape),
            key_spec,
            value_spec,
        ],
        out_specs=(whole(queries.shape), key_spec, value_spec),
        scratch_shapes=[
            pltpu.VMEM((chunks, count, block_rows, 2 * key_wide + value_wide), jnp.bfloat16),
            pltpu.VMEM((count, block_rows, lanes), jnp.float32),
            pltpu.VMEM((lanes, count * block_rows), jnp.float32),
            pltpu.VMEM((chunks, count, 2, block_rows, key_wide), jnp.float32),
            pltpu.VMEM((chunks, count, 2, block_rows, key_wide), jnp.bfloat16),
            pltpu.VMEM((chunks, count, 2, block_rows, key_wide), jnp.bfloat16),
            dma((levels, widest, chunks)),
            dma((levels, widest, chunks)),
            dma((levels, widest)),
            dma((levels, widest)),
            dma((levels, widest, chunks)),
            dma((levels, widest, chunks)),
        ],
        compiler_params=pltpu.CompilerParams(
            dimension_semantics=("arbitrary",),
            collective_id=0,
            has_side_effects=True,
            vmem_limit_bytes=48 << 20,
        ),
        name="fused_backward",
    )(lambdas, visits, bounds, text_count, norms, queries, out_grad, outs, keys, frame_value)
    return query_grad.transpose(1, 0, 2), key_grad.transpose(1, 0, 2), value_grad


def solution(mesh):
    both = ("groups", "tokens")
    return jax.shard_map(
        per_device,
        mesh=mesh,
        in_specs=(
            P(both, None, None),
            P(both, None, None),
            P(both, None),
            P(both, None, None),
            P(both, None),
            P(both, None, None),
            P(),
            P("groups", None),
            P("groups"),
            P(),
        ),
        out_specs=(P(both, None, None), P(both, None, None), P(both, None)),
        check_vma=False,
    )
```

time: 66.1 us -> 54.6 us (0.83)
  Pallas kernels: 52.1 us -> 40.5 us
    pallas_call x1, Pallas kernels: 52.1 us -> 40.5 us  [per_device(): pl.pallas_call(functools.partial(fused_kernel, radices, heads, chunks, la...]
where the time goes in v3:
time: 54.6 us; the launch traced here: 54.3 us
  Pallas kernels  40.5 us (74%)
  local copies, waits for them, and re-layouts  12.4 us (23%)
  between operations  1.34 us (2%)
    pallas_call x1, Pallas kernels, per_device(): pl.pallas_call(functools.partial(fused_kernel, radices, heads, chunks, la...  40.5 us
    unnamed x14, local copies, waits for them, and re-layouts  11.6 us

profile of v3, /device:TPU:0, one launch (start us, length us, event | category | flops | bytes accessed | tf_op | source)
XLA Modules:
  0.0 54.3 jit_solution(11306565197285779669)
XLA Ops:
  1.3 0.8 %reshape.9 = f32[8,20]{1,0:T(8,128)S(1)} reshape(f32[8,2,10]{2,1,0:T(2,128)} %param.15) | data formatting | bytes 1280 | tf_op jit(solution)/shard_map/reshape | solution.py:272
  2.1 0.8 %copy.23 = bf16[8,2,1280]{2,0,1:T(8,128)(2,1)S(1)} copy(bf16[8,2,1280]{2,1,0:T(2,128)(2,1)} %param.10) | data formatting | bytes 81920 | tf_op args[0]
  2.8 0.9 %copy.22 = bf16[8,2,2560]{2,0,1:T(8,128)(2,1)S(1)} copy(bf16[8,2,2560]{2,1,0:T(2,128)(2,1)} %param.13) | data formatting | bytes 163840 | tf_op args[3]
  3.7 0.0 copy-start
  3.8 0.0 copy-start.1
  3.8 0.0 copy-start.2
  3.8 0.0 copy-start.3
  3.8 3.6 %copy.21 = bf16[512,2,1280]{2,0,1:T(8,128)(2,1)} copy(bf16[512,2,1280]{2,1,0:T(2,128)(2,1)} %param.11) | data formatting | bytes 5242880 | tf_op args[1]
  7.4 0.0 copy-done
  7.4 0.0 copy-done.1
  7.4 0.0 copy-done.2
  7.4 0.0 copy-done.3
  7.4 40.5 %fused_backward.1 = (bf16[2,8,1280]{2,1,0:T(8,128)(2,1)S(1)}, bf16[2,512,1280]{2,1,0:T(8,128)(2,1)S(1)}, bf16[512,2560]{1,0:T(8,128)(2,1)S(1)}) custom-call(f32[10]{0:T(128)S(1)} %copy-done.2, s32[16,12]{1,0:T(8,128)S(1)} %copy-done.1, s32[16]{0:T(128)S(1)} %copy-done.3, s32[1]{0:T(128)S(6)} %copy.25.count_ref, f32[8,128]{1,0:T(8,128)S(1)} %pad.4.norm_ref, ...), custom_call_target="tpu_custom_call" | custom-call | tf_op jit(solution)/shard_map/fused_backward/pallas_call | solution.py:288
  47.9 0.6 %copy.16 = bf16[8,2,1280]{2,1,0:T(2,128)(2,1)} copy(bf16[8,2,1280]{2,0,1:T(8,128)(2,1)S(1)} %bitcast.14) | data formatting | bytes 81920
  48.6 4.2 %copy.17 = bf16[512,2,1280]{2,1,0:T(2,128)(2,1)} copy(bf16[512,2,1280]{2,0,1:T(8,128)(2,1)S(1)} %bitcast.11) | data formatting | bytes 5242880
  52.8 1.5 %copy.26 = bf16[512,2560]{1,0:T(8,128)(2,1)} copy(bf16[512,2560]{1,0:T(8,128)(2,1)S(1)} %get-tuple-element.17) | data formatting | bytes 5242880
  (1 shorter events, 0.0 us)
Async XLA Ops:
  3.7 3.6 %copy-start = (bf16[8,2560]{1,0:T(8,128)(2,1)S(1)}, bf16[8,2560]{1,0:T(8,128)(2,1)}, u32[]{:S(2)}) copy-start(bf16[8,2560]{1,0:T(8,128)(2,1)} %g_in.1) | copy-start | bytes 122884
  3.8 3.6 %copy-start.1 = (s32[16,12]{1,0:T(8,128)S(1)}, s32[16,12]{1,0:T(8,128)}, u32[]{:S(2)}) copy-start(s32[16,12]{1,0:T(8,128)} %visit_ref.1) | copy-start | bytes 2308
  3.8 3.6 %copy-start.2 = (f32[10]{0:T(128)S(1)}, f32[10]{0:T(128)}, u32[]{:S(2)}) copy-start(f32[10]{0:T(128)} %lambda_ref.1) | copy-start | bytes 124
  3.8 3.6 %copy-start.3 = (s32[16]{0:T(128)S(1)}, s32[16]{0:T(128)}, u32[]{:S(2)}) copy-start(s32[16]{0:T(128)} %bound_ref.1) | copy-start | bytes 196
